TPU v7x, 32 devices: a whole 2x2x4 slice. The times are simulated.
32 devices in a mesh: dp: 8 (over z, core), tensor: 4 (over y, x).
Axes of the slice: x: 2, y: 2, z: 4, core: 2. Of those that a mesh axis runs over, the one named last changes fastest.
Arguments:
- tokens: bfloat16 [2048, 4096], P('dp', 'tensor'), may hold values from -6 to 6
- cotangent: bfloat16 [2048, 4096], P('dp', 'tensor'), may hold values from -6 to 6
- gate_weight: bfloat16 [4096, 14336], P('dp', 'tensor'), may hold values from -0.09375 to 0.09375
- up_weight: bfloat16 [4096, 14336], P('dp', 'tensor'), may hold values from -0.09375 to 0.09375
- down_weight: bfloat16 [14336, 4096], P('tensor', 'dp'), may hold values from -0.046875 to 0.046875
- counts: int32 [8], replicated, may hold values from 0 to 16, as said below
Outputs:
- outputs: bfloat16 [2048, 4096], P('dp', 'tensor')
- input_grads: bfloat16 [2048, 4096], P('dp', 'tensor')
Inputs may be any that keep to these rules, and one draw needn't show every extreme that they name: counts[r] is the number of live 16-row blocks at the head of rank r's buffer; counts[r] + counts[(r + 4) % 8] = 16 for every rank r, some rank has 16 and some rank has 0.
All inputs are finite; a program needn't handle non-finite values.
Results may differ from a plain program's by a relative error of at most 0.005.
Values may be sent and summed in bfloat16 or wider, within the bound.
A program may use at most 192 MiB of HBM per device.

v0:
```python
import jax
import jax.numpy as jnp
from jax import lax
from jax.sharding import PartitionSpec as P

BLOCK = 16


def passed_along(block, axis, distance):
    devices = range(lax.axis_size(axis))
    route = [((i - distance) % len(devices), i) for i in devices]
    return lax.ppermute(block, axis, route)


def transposed(left, right):
    return lax.dot_general(
        left, right, (((1,), (1,)), ((), ())), preferred_element_type=jnp.float32
    )


def mlp_rows(rows_x, rows_dy, live_rows, gate_full, up_full, down_full):
    whole_x, whole_dy = (
        lax.all_gather(rows_x, "tensor", axis=1, tiled=True),
        lax.all_gather(rows_dy, "tensor", axis=1, tiled=True),
    )
    gate_pre = jnp.dot(whole_x, gate_full, preferred_element_type=jnp.float32)
    up_pre = jnp.dot(whole_x, up_full, preferred_element_type=jnp.float32)
    sigmoid_gate = jax.nn.sigmoid(gate_pre)
    activated = gate_pre * sigmoid_gate
    hidden = (activated * up_pre).astype(jnp.bfloat16)
    partial_y = jnp.dot(hidden, down_full, preferred_element_type=jnp.float32)
    out_rows = lax.psum_scatter(partial_y, "tensor", scatter_dimension=1, tiled=True)
    grad_hidden = transposed(whole_dy, down_full)
    grad_gate = (
        grad_hidden * up_pre * sigmoid_gate * (1.0 + gate_pre * (1.0 - sigmoid_gate))
    ).astype(jnp.bfloat16)
    grad_up = (grad_hidden * activated).astype(jnp.bfloat16)
    partial_dx = transposed(grad_gate, gate_full) + transposed(grad_up, up_full)
    grad_rows = lax.psum_scatter(partial_dx, "tensor", scatter_dimension=1, tiled=True)
    row_mask = live_rows[:, None]
    return ((out_rows * row_mask).astype(jnp.bfloat16), (grad_rows * row_mask).astype(jnp.bfloat16))


def per_device(tokens, cotangent, gate_weight, up_weight, down_weight, counts):
    gate_full, up_full, down_full = (
        lax.all_gather(gate_weight, "dp", axis=0, tiled=True),
        lax.all_gather(up_weight, "dp", axis=0, tiled=True),
        lax.all_gather(down_weight, "dp", axis=1, tiled=True),
    )
    rank_count = lax.axis_size("dp")
    my_rank = lax.axis_index("dp")
    blocks = tokens.shape[0] // BLOCK
    columns = tokens.shape[1]
    own_blocks = counts[my_rank]
    share = blocks // 2
    half_ranks = rank_count // 2
    partner_count = counts[(my_rank + half_ranks) % rank_count]
    upper_x = tokens[share * BLOCK :]
    upper_dy = cotangent[share * BLOCK :]
    got_x, got_dy = passed_along((upper_x, upper_dy), "dp", half_ranks)
    keep_blocks = jnp.minimum(own_blocks, share)
    slot_ids = jnp.arange(share, dtype=jnp.int32)
    foreign = slot_ids - own_blocks
    mine = slot_ids < keep_blocks
    valid = mine | (foreign >= 0) & (foreign < partner_count - share)
    source_index = jnp.where(mine, slot_ids, share + jnp.clip(foreign, 0, share - 1))

    def assemble(lower, received):
        stacked = jnp.concatenate(
            [lower.reshape(share, BLOCK, columns), received.reshape(share, BLOCK, columns)], axis=0
        )
        pieces = jnp.take(stacked, source_index, axis=0)
        pieces = jnp.where(valid[:, None, None], pieces, jnp.zeros_like(pieces))
        return pieces.reshape(share * BLOCK, columns)

    work_x = assemble(tokens[: share * BLOCK], got_x)
    work_dy = assemble(cotangent[: share * BLOCK], got_dy)
    live_rows = jnp.repeat(valid.astype(jnp.float32), BLOCK)
    out_rows, grad_rows = mlp_rows(work_x, work_dy, live_rows, gate_full, up_full, down_full)
    back_pos = own_blocks + slot_ids
    back_ok = back_pos < share
    back_index = jnp.clip(back_pos, 0, share - 1)

    def send_back(source):
        pieces = jnp.take(source.reshape(share, BLOCK, columns), back_index, axis=0)
        pieces = jnp.where(back_ok[:, None, None], pieces, jnp.zeros_like(pieces))
        return pieces.reshape(share * BLOCK, columns)

    back_out, back_grad = passed_along(
        (send_back(out_rows), send_back(grad_rows)), "dp", half_ranks
    )
    upper_live = slot_ids < own_blocks - share

    def home_rows(worked, returned_rows):
        lower = jnp.where(
            mine[:, None, None],
            worked.reshape(share, BLOCK, columns),
            jnp.zeros((share, BLOCK, columns), worked.dtype),
        )
        upper = jnp.where(
            upper_live[:, None, None],
            returned_rows.reshape(share, BLOCK, columns),
            jnp.zeros((share, BLOCK, columns), worked.dtype),
        )
        return jnp.concatenate([lower, upper], axis=0).reshape(blocks * BLOCK, columns)

    outputs = home_rows(out_rows, back_out)
    input_grads = home_rows(grad_rows, back_grad)
    return (outputs, input_grads)


def solution(mesh):
    in_specs = (
        P("dp", "tensor"),
        P("dp", "tensor"),
        P("dp", "tensor"),
        P("dp", "tensor"),
        P("tensor", "dp"),
        P(),
    )
    out_specs = (P("dp", "tensor"), P("dp", "tensor"))
    return jax.shard_map(
        per_device, mesh=mesh, in_specs=in_specs, out_specs=out_specs, check_vma=False
    )
```

profile of v0, /device:TPU:0, one launch (start us, length us, event | category | flops | bytes accessed | tf_op | source)
XLA Modules:
  0.0 1015.0 jit_solution(16153699752031720627)
XLA Ops:
  7.2 0.0 all-gather.6.cloned.1.call-start
  7.2 1.1 fusion.12
  8.3 4.1 collective-permute-start
  12.4 1.1 fusion.11
  13.5 0.1 collective-permute-start.2
  13.6 0.6 fusion.13
  15.5 0.6 compare_and_fusion.1
  16.2 14.7 %collective-permute-done = bf16[128,1024]{1,0:T(8,128)(2,1)S(1)} collective-permute-done((bf16[128,1024]{1,0:T(8,128)(2,1)S(1)}, bf16[128,1024]{1,0:T(8,128)(2,1)S(1)}, u32[]{:S(2)}, u32[]{:S(2)}) %collective-permute-start) | collective-permute-done | bytes 262176 | tf_op jit(solution)/shard_map/ppermute | solution.py:12
  30.9 0.6 gather_fusion
  31.4 4.1 collective-permute-done.2
  35.6 0.6 gather_fusion.2
  36.2 0.9 select_select_fusion.1
  37.2 0.0 all-gather.10.cloned.1.call-start
  37.2 0.7 all-gather.10.cloned.1.call-update
  38.0 0.7 all-gather.8.cloned.1.call-update
  38.7 0.5 all-gather.14.cloned.1.call-update
  39.3 0.5 all-gather.12.cloned.1.call-update
  39.8 0.0 reduce-scatter.5.cloned.1.call-start
  39.9 25.1 %all-gather.6.cloned.1.call-done = bf16[128,4096]{1,0:T(8,128)(2,1)} async-done(((bf16[128,1024]{1,0:T(8,128)(2,1)}), bf16[128,4096]{1,0:T(8,128)(2,1)}) %all-gather.6.cloned.1.call-update) | async-done | bytes 1048592 | tf_op jit(solution)/shard_map/all_gather | solution.py:23
  65.0 255.9 %all-gather.10.cloned.1.call-done = bf16[4096,3584]{1,0:T(8,128)(2,1)} async-done(((bf16[512,3584]{1,0:T(8,128)(2,1)}), bf16[4096,3584]{1,0:T(8,128)(2,1)}) %all-gather.10.cloned.1.call-update) | async-done | bytes 29360144 | tf_op jit(solution)/shard_map/all_gather | solution.py:47
  320.9 16.9 %fusion.15 = f32[128,3584]{1,0:T(8,128)} fusion(bf16[128,4096]{1,0:T(8,128)(2,1)} %all-gather.6.cloned.1.call-done, bf16[4096,3584]{1,0:T(8,128)(2,1)} %all-gather.10.cloned.1.call-done), kind=kOutput, calls=%fused_computation.47 | convolution fusion | flops 3758096384 | bytes 32243712 | tf_op jit(solution)/shard_map/dot_general | solution.py:27
  337.8 237.2 %all-gather.8.cloned.1.call-done = bf16[4096,3584]{1,0:T(8,128)(2,1)} async-done(((bf16[512,3584]{1,0:T(8,128)(2,1)}), bf16[4096,3584]{1,0:T(8,128)(2,1)}) %all-gather.8.cloned.1.call-update) | async-done | bytes 29360144 | tf_op jit(solution)/shard_map/all_gather | solution.py:46
  575.0 11.7 %fusion.14 = f32[128,3584]{1,0:T(8,128)S(1)} fusion(bf16[128,4096]{1,0:T(8,128)(2,1)S(1)} %copy-done.1, bf16[4096,3584]{1,0:T(8,128)(2,1)} %all-gather.8.cloned.1.call-done), kind=kOutput, calls=%fused_computation.46 | convolution fusion | flops 3758096384 | bytes 32243712 | tf_op jit(solution)/shard_map/dot_general | solution.py:26
  586.7 15.3 %all-gather.14.cloned.1.call-done = bf16[128,4096]{1,0:T(8,128)(2,1)} async-done(((bf16[128,1024]{1,0:T(8,128)(2,1)}), bf16[128,4096]{1,0:T(8,128)(2,1)}) %all-gather.14.cloned.1.call-update) | async-done | bytes 1048592 | tf_op jit(solution)/shard_map/all_gather | solution.py:24
  602.0 255.7 %all-gather.12.cloned.1.call-done = bf16[3584,4096]{1,0:T(8,128)(2,1)} async-done(((bf16[3584,512]{1,0:T(8,128)(2,1)}), bf16[3584,4096]{1,0:T(8,128)(2,1)}) %all-gather.12.cloned.1.call-update) | async-done | bytes 29360144 | tf_op jit(solution)/shard_map/all_gather | solution.py:48
  857.7 16.2 %fusion.16 = f32[128,3584]{1,0:T(8,128)} fusion(bf16[128,4096]{1,0:T(8,128)(2,1)} %all-gather.14.cloned.1.call-done, bf16[3584,4096]{1,0:T(8,128)(2,1)} %all-gather.12.cloned.1.call-done), kind=kOutput, calls=%fused_computation.48 | convolution fusion | flops 3758096384 | bytes 32243712 | tf_op jit(solution)/shard_map/dot_general | solution.py:16
  873.9 17.0 %fusion.2 = f32[128,4096]{1,0:T(8,128)S(1)} fusion(bf16[4096,3584]{1,0:T(8,128)(2,1)} %all-gather.8.cloned.1.call-done, f32[128,3584]{1,0:T(8,128)S(1)} %fusion.14, f32[128,3584]{1,0:T(8,128)} %fusion.16, f32[128,3584]{1,0:T(8,128)} %fusion.15), kind=kOutput, calls=%fused_computation.11 | convolution fusion | flops 3762683904 | bytes 36962304 | tf_op jit(solution)/shard_map/dot_general | solution.py:16
  890.9 15.4 %convolution_add_fusion = f32[128,4096]{1,0:T(8,128)} fusion(f32[128,4096]{1,0:T(8,128)S(1)} %fusion.2, bf16[4096,3584]{1,0:T(8,128)(2,1)} %all-gather.10.cloned.1.call-done, f32[128,3584]{1,0:T(8,128)S(1)} %copy-done, f32[128,3584]{1,0:T(8,128)S(1)} %fusion.14), kind=kOutput, calls=%fused_computation.4 | convolution fusion | flops 3761373184 | bytes 37224448 | tf_op jit(solution)/shard_map/dot_general | solution.py:16
  906.4 0.3 reduce-scatter.3.cloned.1.call-start
  906.7 15.8 %fusion.1 = f32[128,4096]{1,0:T(8,128)} fusion(bf16[3584,4096]{1,0:T(8,128)(2,1)} %all-gather.12.cloned.1.call-done, f32[128,3584]{1,0:T(8,128)} %fusion.15, f32[128,3584]{1,0:T(8,128)S(1)} %fusion.14), kind=kOutput, calls=%fused_computation.10 | convolution fusion | flops 3760848896 | bytes 35127296 | tf_op jit(solution)/shard_map/dot_general | solution.py:31
  922.5 0.1 broadcast_in_dim.66
  922.6 0.1 mul.39
  923.3 0.6 compare_select_fusion
  923.9 0.6 compare_and_fusion
  924.6 15.3 %reduce-scatter.5.cloned.1.call-done = f32[128,1024]{1,0:T(8,128)} async-done(((f32[128,4096]{1,0:T(8,128)}), f32[128,1024]{1,0:T(8,128)}) %reduce-scatter.5.cloned.1.call-update) | async-done | bytes 524304 | tf_op jit(solution)/shard_map/reduce_scatter | solution.py:39
  939.9 38.2 %reduce-scatter.3.cloned.1.call-done = f32[128,1024]{1,0:T(8,128)} async-done(((f32[128,4096]{1,0:T(8,128)}), f32[128,1024]{1,0:T(8,128)}) %reduce-scatter.3.cloned.1.call-update) | async-done | bytes 524304 | tf_op jit(solution)/shard_map/reduce_scatter | solution.py:32
  978.1 1.3 multiply_convert_fusion.6
  979.4 0.6 gather_fusion.1
  980.0 0.6 gather_fusion.3
  980.5 0.1 select_select_fusion
  980.7 2.5 collective-permute-start.3
  983.2 0.5 collective-permute-start.1
  983.7 0.1 broadcast_select_fusion.2
  983.8 18.0 %collective-permute-done.3 = bf16[128,1024]{1,0:T(8,128)(2,1)S(1)} collective-permute-done((bf16[128,1024]{1,0:T(8,128)(2,1)S(1)}, bf16[128,1024]{1,0:T(8,128)(2,1)S(1)}, u32[]{:S(2)}, u32[]{:S(2)}) %collective-permute-start.3) | collective-permute-done | bytes 262176 | tf_op jit(solution)/shard_map/ppermute | solution.py:12
  1001.8 4.6 collective-permute-done.1
  1006.4 0.1 broadcast_select_fusion
  1006.5 0.8 pad_maximum_fusion.3
  1007.4 0.8 pad_maximum_fusion.1
  (18 shorter events, 0.3 us)
Async XLA Ops:
  7.2 6.4 copy-start.2
  7.2 57.8 %all-gather.6.cloned.1.call-start = ((), (), s32[]{:S(2)}) async-start(), calls=%async_computation.2 | async-start | bytes 1310720 | tf_op jit(solution)/shard_map/all_gather | solution.py:23
  8.3 22.5 %collective-permute-start = (bf16[128,1024]{1,0:T(8,128)(2,1)S(1)}, bf16[128,1024]{1,0:T(8,128)(2,1)S(1)}, u32[]{:S(2)}, u32[]{:S(2)}) collective-permute-start(bf16[128,1024]{1,0:T(8,128)(2,1)S(1)} %get-tuple-element.11), channel_id=1, source_target_pairs={{16,0},{20,4},{24,8},{28,12},{0,16},{4,20},{8,24},{12,28},{17,1},{... | collective-permute-start | bytes 786440 | tf_op jit(solution)/shard_map/ppermute | solution.py:12
  13.5 22.1 %collective-permute-start.2 = (bf16[128,1024]{1,0:T(8,128)(2,1)S(1)}, bf16[128,1024]{1,0:T(8,128)(2,1)S(1)}, u32[]{:S(2)}, u32[]{:S(2)}) collective-permute-start(bf16[128,1024]{1,0:T(8,128)(2,1)S(1)} %get-tuple-element.9), channel_id=1, source_target_pairs={{16,0},{20,4},{24,8},{28,12},{0,16},{4,20},{8,24},{12,28},{17,1},{... | collective-permute-start | bytes 786440 | tf_op jit(solution)/shard_map/ppermute | solution.py:12
  37.2 283.7 %all-gather.10.cloned.1.call-start = ((), (), s32[]{:S(2)}) async-start(), calls=%async_computation.4 | async-start | bytes 33030144 | tf_op jit(solution)/shard_map/all_gather | solution.py:47
  37.9 537.1 %all-gather.8.cloned.1.call-start = ((), (), s32[]{:S(2)}) async-start(), calls=%async_computation.3 | async-start | bytes 33030144 | tf_op jit(solution)/shard_map/all_gather | solution.py:46
  38.6 563.3 %all-gather.14.cloned.1.call-start = ((), (), s32[]{:S(2)}) async-start(), calls=%async_computation.7 | async-start | bytes 1310720 | tf_op jit(solution)/shard_map/all_gather | solution.py:24
  39.2 818.5 %all-gather.12.cloned.1.call-start = ((), (), s32[]{:S(2)}) async-start(), calls=%async_computation.5 | async-start | bytes 33030144 | tf_op jit(solution)/shard_map/all_gather | solution.py:48
  39.8 900.1 %reduce-scatter.5.cloned.1.call-start = ((), (), s32[]{:S(2)}) async-start(), calls=%async_computation.8 | async-start | bytes 2621440 | tf_op jit(solution)/shard_map/reduce_scatter | solution.py:39
  65.0 510.0 %copy-start.1 = (bf16[128,4096]{1,0:T(8,128)(2,1)S(1)}, bf16[128,4096]{1,0:T(8,128)(2,1)}, u32[]{:S(2)}) copy-start(bf16[128,4096]{1,0:T(8,128)(2,1)} %all-gather.6.cloned.1.call-done) | copy-start | bytes 3145732
  873.9 17.0 %copy-start = (f32[128,3584]{1,0:T(8,128)S(1)}, f32[128,3584]{1,0:T(8,128)}, u32[]{:S(2)}) copy-start(f32[128,3584]{1,0:T(8,128)} %fusion.16) | copy-start | bytes 5505028
  906.4 71.7 %reduce-scatter.3.cloned.1.call-start = ((), (), s32[]{:S(2)}) async-start(), calls=%async_computation.6 | async-start | bytes 2621440 | tf_op jit(solution)/shard_map/reduce_scatter | solution.py:32
  980.7 21.1 %collective-permute-start.3 = (bf16[128,1024]{1,0:T(8,128)(2,1)S(1)}, bf16[128,1024]{1,0:T(8,128)(2,1)S(1)}, u32[]{:S(2)}, u32[]{:S(2)}) collective-permute-start(bf16[128,1024]{1,0:T(8,128)(2,1)S(1)} %bitcast.36), channel_id=1, source_target_pairs={{16,0},{20,4},{24,8},{28,12},{0,16},{4,20},{8,24},{12,28},{17,1},{... | collective-permute-start | bytes 786440 | tf_op jit(solution)/shard_map/ppermute | solution.py:12
  983.2 23.2 %collective-permute-start.1 = (bf16[128,1024]{1,0:T(8,128)(2,1)S(1)}, bf16[128,1024]{1,0:T(8,128)(2,1)S(1)}, u32[]{:S(2)}, u32[]{:S(2)}) collective-permute-start(bf16[128,1024]{1,0:T(8,128)(2,1)S(1)} %bitcast.35), channel_id=1, source_target_pairs={{16,0},{20,4},{24,8},{28,12},{0,16},{4,20},{8,24},{12,28},{17,1},{... | collective-permute-start | bytes 786440 | tf_op jit(solution)/shard_map/ppermute | solution.py:12
Sparse Core Ops, SparseCore 0:
  37.3 27.6 all-gather.5
  66.6 254.2 all-gather.9
  322.5 252.3 all-gather.7
  577.3 24.6 all-gather.13
  603.4 254.2 all-gather.11
  906.5 33.3 reduce-scatter.4
  942.9 35.1 reduce-scatter.2
where the time goes:
time: 1020 us
  waiting for transfers between devices  887 us (87%)
  matrix products  93.1 us (9%)
  between operations  16.2 us (2%)
    all_gather x1, waiting for transfers between devices, per_device(): lax.all_gather(up_weight, 'dp', axis=0, tiled=True)  256 us
    all_gather x1, waiting for transfers between devices, per_device(): lax.all_gather(down_weight, 'dp', axis=1, tiled=True)  256 us
    all_gather x1, waiting for transfers between devices, per_device(): lax.all_gather(gate_weight, 'dp', axis=0, tiled=True)  237 us
    dot_general x3, matrix products, transposed(): lax.dot_general(left, right, (((1,), (1,)), ((), ())), preferred_element_...  48.7 us
    ppermute x4, waiting for transfers between devices, passed_along(): return lax.ppermute(block, axis, route)  41.4 us
    reduce_scatter x1, waiting for transfers between devices, mlp_rows(): lax.psum_scatter(partial_y, 'tensor', scatter_dimension=1, tiled=True)  38.2 us
    all_gather x1, waiting for transfers between devices, mlp_rows(): lax.all_gather(rows_x, 'tensor', axis=1, tiled=True)  25.1 us
  transfers between devices with their start and end apart: 11, of which 11 were waited for; matrix products, arithmetic and copies ran while one was open for 5% of the time, Pallas kernels for 0%

commit v1 on v0

v1 whole, which is shorter than its diff:
```python
import jax
import jax.numpy as jnp
from jax import lax
from jax.sharding import PartitionSpec as P

BLOCK = 16
CORES = 2


def transposed(left, right):
    return lax.dot_general(
        left, right, (((1,), (1,)), ((), ())), preferred_element_type=jnp.float32
    )


def matmul(left, right):
    return jnp.dot(left, right, preferred_element_type=jnp.float32)


def per_device(tokens, cotangent, gate_weight, up_weight, down_weight, counts):
    ranks = lax.axis_size("dp")
    tensors = lax.axis_size("tensor")
    chips = ranks // CORES
    half = chips // 2
    me = lax.axis_index("dp")
    core = me % CORES
    chip = me // CORES
    planes = [[z * CORES + c for z in range(chips)] for c in range(CORES)]
    rows, features = tokens.shape
    blocks = rows // BLOCK
    width, units = gate_weight.shape
    model = width * ranks
    part = units // chips

    def over_chips(pieces):
        return lax.all_to_all(pieces, "dp", 0, 0, tiled=True, axis_index_groups=planes)

    def swapped(block):
        return lax.ppermute(block, "dp", [(i, i ^ 1) for i in range(ranks)])

    both = jnp.concatenate([tokens, cotangent], axis=1)
    stacked = lax.all_gather(both, "dp", axis=0, tiled=True, axis_index_groups=planes)
    stacked = stacked.reshape(chips * blocks, BLOCK, 2 * features)
    slot = jnp.arange(blocks, dtype=jnp.int32)
    lower = jnp.arange(half, dtype=jnp.int32)
    lower_count = counts[lower * CORES + core][:, None]
    source = jnp.where(
        slot[None] < lower_count,
        lower[:, None] * blocks + slot[None],
        (lower[:, None] + half) * blocks + slot[None] - lower_count,
    ).reshape(-1)
    packed = jnp.take(stacked, source, axis=0).reshape(half * rows, 2 * features)
    work = half * rows
    whole_x = lax.all_gather(packed[:, :features], "tensor", axis=1, tiled=True)
    whole_dy = lax.all_gather(packed[:, features:], "tensor", axis=1, tiled=True)

    def by_core(whole):
        whole = whole.reshape(work, chips, CORES, width)
        zero, one = (whole[:, :, c].reshape(work, chips * width) for c in range(CORES))
        return jnp.where(core == 0, zero, one), jnp.where(core == 0, one, zero)

    x_own, x_far = by_core(whole_x)
    dy_own, dy_far = by_core(whole_dy)

    def rows_first(weight):
        pieces = weight.reshape(width, chips, part).transpose(1, 0, 2)
        return over_chips(pieces).reshape(chips * width, part)

    gate_own = rows_first(gate_weight)
    up_own = rows_first(up_weight)
    down_own = over_chips(down_weight.reshape(chips, part, width))
    gate_far, up_far, down_far = swapped(gate_own), swapped(up_own), swapped(down_own)

    def grad_in(left, right):
        left = left.reshape(work, chips, width)
        return lax.dot_general(
            left, right, (((1, 2), (0, 2)), ((), ())), preferred_element_type=jnp.float32
        )

    gate_pre = matmul(x_own, gate_own) + matmul(x_far, gate_far)
    up_pre = matmul(x_own, up_own) + matmul(x_far, up_far)
    sigmoid_gate = jax.nn.sigmoid(gate_pre)
    activated = gate_pre * sigmoid_gate
    hidden = (activated * up_pre).astype(jnp.bfloat16)
    grad_hidden = grad_in(dy_own, down_own) + grad_in(dy_far, down_far)
    grad_gate = (
        grad_hidden * up_pre * sigmoid_gate * (1.0 + gate_pre * (1.0 - sigmoid_gate))
    ).astype(jnp.bfloat16)
    grad_up = (grad_hidden * activated).astype(jnp.bfloat16)

    def out_part(down):
        result = lax.dot_general(
            hidden, down, (((1,), (1,)), ((), ())), preferred_element_type=jnp.float32
        )
        return result.astype(jnp.bfloat16).reshape(work, chips, width)

    def grad_part(gate, up):
        result = transposed(grad_gate, gate) + transposed(grad_up, up)
        return result.astype(jnp.bfloat16).reshape(work, chips, width)

    def whole_features(own, far):
        zero = jnp.where(core == 0, own, far)
        one = jnp.where(core == 0, far, own)
        return jnp.stack([zero, one], axis=2).reshape(work, model)

    def reduced(partial):
        pieces = partial.reshape(work, tensors, features).transpose(1, 0, 2)
        got = lax.all_to_all(pieces, "tensor", 0, 0, tiled=True)
        total = jnp.sum(got.astype(jnp.float32), axis=0).astype(jnp.bfloat16)
        pieces = total.reshape(half, 2, rows // 2, features).transpose(1, 0, 2, 3)
        pieces = pieces.reshape(chips, rows // 2, features)
        got = over_chips(pieces)
        return jnp.sum(got.astype(jnp.float32), axis=0).astype(jnp.bfloat16)

    out_rows = reduced(whole_features(out_part(down_own), out_part(down_far)))
    grad_rows = reduced(
        whole_features(grad_part(gate_own, up_own), grad_part(gate_far, up_far))
    )

    done = jnp.concatenate([out_rows, grad_rows], axis=1)
    route = [(i, (i + ranks // 2) % ranks) for i in range(ranks)]
    other = lax.ppermute(done, "dp", route)
    is_lower = chip < half
    pair = jnp.where(
        is_lower, jnp.concatenate([done, other]), jnp.concatenate([other, done])
    ).reshape(blocks, BLOCK, 2 * features)
    first = jnp.where(is_lower, 0, blocks - counts[me])
    home = jnp.take(pair, jnp.minimum(first + slot, blocks - 1), axis=0)
    home = jnp.where((slot < counts[me])[:, None, None], home, jnp.zeros_like(home))
    home = home.reshape(rows, 2 * features)
    return home[:, :features], home[:, features:]


def solution(mesh):
    in_specs = (
        P("dp", "tensor"),
        P("dp", "tensor"),
        P("dp", "tensor"),
        P("dp", "tensor"),
        P("tensor", "dp"),
        P(),
    )
    out_specs = (P("dp", "tensor"), P("dp", "tensor"))
    return jax.shard_map(
        per_device, mesh=mesh, in_specs=in_specs, out_specs=out_specs, check_vma=False
    )
```

time: 1020 us -> 604 us (0.59)
  waiting for transfers between devices: 887 us -> 420 us
  local copies, waits for them, and re-layouts: 5.19 us -> 64.7 us
  matrix products: 93.1 us -> 50.2 us
  starting transfers between devices: 7.7 us -> 33.8 us
  other arithmetic: 6.28 us -> 18.4 us
    all_gather x5 -> x3, waiting for transfers between devices: 789 us -> 142 us  [the longest x1 142 us: per_device(): lax.all_gather(both, 'dp', axis=0, tiled=True, axis_index_groups=planes)]
    all_to_all x0 -> x7, waiting for transfers between devices: none -> 257 us  [the longest x5 195 us: over_chips(): lax.all_to_all(pieces, 'dp', 0, 0, tiled=True, axis_index_groups=planes)]
    reduce_scatter x2 -> x0, waiting for transfers between devices: 53.5 us -> none  [the longest x1 38.2 us: mlp_rows(): lax.psum_scatter(partial_y, 'tensor', scatter_dimension=1, tiled=True)]
    all_to_all x0 -> x7, starting transfers between devices: none -> 33.1 us  [the longest x5 23.1 us: over_chips(): lax.all_to_all(pieces, 'dp', 0, 0, tiled=True, axis_index_groups=planes)]
    dot_general x3 -> x4, matrix products: 48.7 us -> 17.9 us  [transposed(): lax.dot_general(left, right, (((1,), (1,)), ((), ())), preferred_element_...]
    ppermute x4, waiting for transfers between devices: 41.4 us -> 20.7 us  [the longest x1 20.7 us: per_device(): other = lax.ppermute(done, 'dp', route)]
    all_gather x0 -> x2, local copies, waits for them, and re-layouts: none -> 13 us  [the longest x1 6.51 us: per_device(): lax.all_gather(packed[:, features:], 'tensor', axis=1, tiled=True)]
    unnamed x6 -> x12, local copies, waits for them, and re-layouts: 0.01 us -> 12.6 us
  transfers between devices with their start and end apart: 11 -> 14, of which waited for: 11 -> 8; matrix products, arithmetic and copies ran while one was open for 5% -> 18% of each run, Pallas kernels for 0% -> 0%
where the time goes in v1:
time: 604 us; the launch traced here: 602 us
  waiting for transfers between devices  420 us (70%)
  local copies, waits for them, and re-layouts  64.7 us (11%)
  matrix products  50.2 us (8%)
  starting transfers between devices  33.8 us (6%)
  other arithmetic  18.4 us (3%)
  between operations  14.8 us (2%)
    all_to_all x5, waiting for transfers between devices, over_chips(): lax.all_to_all(pieces, 'dp', 0, 0, tiled=True, axis_index_groups=planes)  195 us
    all_gather x1, waiting for transfers between devices, per_device(): lax.all_gather(both, 'dp', axis=0, tiled=True, axis_index_groups=planes)  142 us
    all_to_all x2, waiting for transfers between devices, reduced(): got = lax.all_to_all(pieces, 'tensor', 0, 0, tiled=True)  61.7 us
    all_to_all x5, starting transfers between devices, over_chips(): lax.all_to_all(pieces, 'dp', 0, 0, tiled=True, axis_index_groups=planes)  23.1 us
    ppermute x1, waiting for transfers between devices, per_device(): other = lax.ppermute(done, 'dp', route)  20.7 us
    dot_general x4, matrix products, transposed(): lax.dot_general(left, right, (((1,), (1,)), ((), ())), preferred_element_...  17.9 us
    dot_general x4, matrix products, matmul(): return jnp.dot(left, right, preferred_element_type=jnp.float32)  14.2 us
    unnamed x12, local copies, waits for them, and re-layouts  12.6 us
  transfers between devices with their start and end apart: 14, of which 8 were waited for; matrix products, arithmetic and copies ran while one was open for 18% of the time, Pallas kernels for 0%

profile of v1, /device:TPU:0, one launch (start us, length us, event | category | flops | bytes accessed | tf_op | source)
XLA Modules:
  0.0 601.8 jit_solution(11762831522302422544)
XLA Ops:
  7.2 2.4 pad_maximum_fusion.2
  9.6 6.1 %copy.39 = bf16[4,896,512]{1,2,0:T(8,128)(2,1)} copy(bf16[4,896,512]{2,1,0:T(8,128)(2,1)} %bitcast.98) | data formatting | bytes 7340032 | tf_op jit(solution)/shard_map/reshape | solution.py:71
  15.7 6.5 %all-to-all-start.2 = ((bf16[4,896,512]{1,2,0:T(8,128)(2,1)}), bf16[4,896,512]{1,2,0:T(8,128)(2,1)}, u32[]{:S(2)}, u32[]{:S(2)}) async-start(bf16[4,896,512]{1,2,0:T(8,128)(2,1)} %copy.39), calls=%async_computation.2 | async-start | bytes 7340032 | tf_op jit(solution)/shard_map/all_to_all | solution.py:36
  23.9 141.8 %all-gather.4.cloned.1.call-done = bf16[1024,2048]{1,0:T(8,128)(2,1)} async-done(((bf16[256,2048]{1,0:T(8,128)(2,1)}), bf16[1024,2048]{1,0:T(8,128)(2,1)}) %all-gather.4.cloned.1.call-update) | async-done | bytes 4194320 | tf_op jit(solution)/shard_map/all_gather | solution.py:42
  165.8 2.9 gather_fusion.1
  169.0 1.5 fusion.20
  170.5 5.9 copy.35
  176.5 4.8 all-to-all-start
  181.3 0.7 all-gather.6.cloned.1.call-update
  182.0 6.0 copy.37
  188.0 74.8 %all-to-all-done = bf16[4,512,896]{1,2,0:T(8,128)(2,1)} async-done(((bf16[4,512,896]{1,2,0:T(8,128)(2,1)}), bf16[4,512,896]{1,2,0:T(8,128)(2,1)}, u32[]{:S(2)}, u32[]{:S(2)}) %all-to-all-start) | async-done | bytes 3670048 | tf_op jit(solution)/shard_map/all_to_all | solution.py:36
  262.8 4.8 all-to-all-start.1
  267.6 6.0 copy.36
  274.1 75.0 %all-to-all-done.1 = bf16[4,512,896]{1,2,0:T(8,128)(2,1)} async-done(((bf16[4,512,896]{1,2,0:T(8,128)(2,1)}), bf16[4,512,896]{1,2,0:T(8,128)(2,1)}, u32[]{:S(2)}, u32[]{:S(2)}) %all-to-all-start.1) | async-done | bytes 3670048 | tf_op jit(solution)/shard_map/all_to_all | solution.py:36
  349.1 6.0 copy.38
  355.1 6.5 %copy.43 = bf16[512,4096]{0,1:T(8,128)(2,1)} copy(bf16[512,4096]{1,0:T(8,128)(2,1)} %all-gather.8.cloned.1.call-done) | data formatting | bytes 8388608 | tf_op jit(solution)/shard_map/all_gather | solution.py:55
  361.6 6.4 %copy.34 = bf16[512,4096]{0,1:T(8,128)(2,1)} copy(bf16[512,4096]{1,0:T(8,128)(2,1)} %all-gather.6.cloned.1.call-done) | data formatting | bytes 8388608 | tf_op jit(solution)/shard_map/all_gather | solution.py:54
  368.1 2.6 broadcast_select_fusion.2
  371.4 2.3 fusion.22
  373.7 2.3 fusion.23
  376.1 4.4 fusion.2
  380.6 4.4 convolution_add_fusion.1
  385.0 4.5 bitcast_add_fusion
  389.5 5.2 fusion.16
  394.6 4.7 convolution_convert_fusion.1
  399.3 4.5 select_bitcast_fusion.1
  404.1 2.5 copy.40
  406.6 4.9 all-to-all-start.3
  411.5 4.4 fusion.24
  415.9 4.6 fusion.25
  420.5 2.4 add_convert_fusion.1
  422.9 6.5 %broadcast_select_fusion.1 = (bf16[512,2048]{1,0:T(8,128)(2,1)}, bf16[512,2048]{1,0:T(8,128)(2,1)}) fusion(bf16[512,2048]{1,0:T(8,128)(2,1)S(1)} %add_convert_fusion.1, pred[]{:T(512)S(6)} %eq.4, f32[512,2048]{1,0:T(8,128)S(1)} %fusion.25, bf16[512,896]{1,0:T(8,128)(2,1)S(1)} %get-tuple-element.9, bf16[2048,896]{1,0:T(8,128)(2,1)} %collective-permute-done), kind=kOutput, calls=%fused_computation.17 | convolution fusion | flops 1883242496 | bytes 15073281 | tf_op jit(solution)/shard_map/dot_general | solution.py:11
  429.5 2.9 copy.56
  432.3 3.9 copy.57
  436.3 4.0 pad_maximum_fusion.1
  440.2 19.6 %all-to-all-done.3 = bf16[4,512,1024]{1,2,0:T(8,128)(2,1)} async-done(((bf16[4,512,1024]{1,2,0:T(8,128)(2,1)}), bf16[4,512,1024]{1,2,0:T(8,128)(2,1)}, u32[]{:S(2)}, u32[]{:S(2)}) %all-to-all-start.3) | async-done | bytes 4194336 | tf_op jit(solution)/shard_map/all_to_all | solution.py:108
  459.9 5.1 all-to-all-start.5
  465.0 3.5 reduce_sum.48
  469.1 1.1 copy.42
  470.1 42.1 %all-to-all-done.5 = bf16[4,512,1024]{1,2,0:T(8,128)(2,1)} async-done(((bf16[4,512,1024]{1,2,0:T(8,128)(2,1)}), bf16[4,512,1024]{1,2,0:T(8,128)(2,1)}, u32[]{:S(2)}, u32[]{:S(2)}) %all-to-all-start.5) | async-done | bytes 4194336 | tf_op jit(solution)/shard_map/all_to_all | solution.py:108
  512.2 3.5 all-to-all-start.4
  515.8 3.5 reduce_sum.50
  519.8 1.0 copy.51
  520.8 20.1 %all-to-all-done.4 = bf16[4,128,1024]{2,1,0:T(8,128)(2,1)S(1)} async-done(((bf16[4,128,1024]{2,1,0:T(8,128)(2,1)}), bf16[4,128,1024]{2,1,0:T(8,128)(2,1)S(1)}, u32[]{:S(2)}, u32[]{:S(2)}) %all-to-all-start.4) | async-done | bytes 1048608 | tf_op jit(solution)/shard_map/all_to_all | solution.py:36
  541.0 3.5 all-to-all-start.6
  544.7 25.0 %all-to-all-done.6 = bf16[4,128,1024]{2,1,0:T(8,128)(2,1)S(1)} async-done(((bf16[4,128,1024]{2,1,0:T(8,128)(2,1)}), bf16[4,128,1024]{2,1,0:T(8,128)(2,1)S(1)}, u32[]{:S(2)}, u32[]{:S(2)}) %all-to-all-start.6) | async-done | bytes 1048608 | tf_op jit(solution)/shard_map/all_to_all | solution.py:36
  572.3 20.7 %collective-permute-done.3 = bf16[128,2048]{1,0:T(8,128)(2,1)S(1)} collective-permute-done((bf16[128,2048]{1,0:T(8,128)(2,1)S(1)}, bf16[128,2048]{1,0:T(8,128)(2,1)S(1)}, u32[]{:S(2)}, u32[]{:S(2)}) %collective-permute-start.3) | collective-permute-done | bytes 524320 | tf_op jit(solution)/shard_map/ppermute | solution.py:122
  594.2 1.0 fusion.21
  (67 shorter events, 8.1 us)
Async XLA Ops:
  7.2 158.6 %all-gather.4.cloned.1.call-start = ((), (), s32[]{:S(2)}) async-start(), calls=%async_computation.7 | async-start | bytes 5242880 | tf_op jit(solution)/shard_map/all_gather | solution.py:42
  15.7 6.5 %copy-start = (s32[8]{0:T(128)S(1)}, s32[8]{0:T(128)}, u32[]{:S(2)}) copy-start(s32[8]{0:T(128)} %param.11) | copy-start | bytes 100
  15.7 160.8 %all-to-all-start.2 = ((bf16[4,896,512]{1,2,0:T(8,128)(2,1)}), bf16[4,896,512]{1,2,0:T(8,128)(2,1)}, u32[]{:S(2)}, u32[]{:S(2)}) async-start(bf16[4,896,512]{1,2,0:T(8,128)(2,1)} %copy.39), calls=%async_computation.2 | async-start | bytes 7340032 | tf_op jit(solution)/shard_map/all_to_all | solution.py:36
  22.1 333.0 %all-gather.8.cloned.1.call-start = ((), (), s32[]{:S(2)}) async-start(), calls=%async_computation.9 | async-start | bytes 5242880 | tf_op jit(solution)/shard_map/all_gather | solution.py:55
  176.5 86.3 %all-to-all-start = ((bf16[4,512,896]{1,2,0:T(8,128)(2,1)}), bf16[4,512,896]{1,2,0:T(8,128)(2,1)}, u32[]{:S(2)}, u32[]{:S(2)}) async-start(bf16[4,512,896]{1,2,0:T(8,128)(2,1)} %bitcast.89), calls=%async_computation | async-start | bytes 7340032 | tf_op jit(solution)/shard_map/all_to_all | solution.py:36
  181.2 180.4 %all-gather.6.cloned.1.call-start = ((), (), s32[]{:S(2)}) async-start(), calls=%async_computation.8 | async-start | bytes 5242880 | tf_op jit(solution)/shard_map/all_gather | solution.py:54
  262.8 86.3 %all-to-all-start.1 = ((bf16[4,512,896]{1,2,0:T(8,128)(2,1)}), bf16[4,512,896]{1,2,0:T(8,128)(2,1)}, u32[]{:S(2)}, u32[]{:S(2)}) async-start(bf16[4,512,896]{1,2,0:T(8,128)(2,1)} %bitcast.90), calls=%async_computation.1 | async-start | bytes 7340032 | tf_op jit(solution)/shard_map/all_to_all | solution.py:36
  273.6 107.0 %collective-permute-start = (bf16[2048,896]{1,0:T(8,128)(2,1)}, bf16[2048,896]{1,0:T(8,128)(2,1)}, u32[]{:S(2)}, u32[]{:S(2)}) collective-permute-start(bf16[2048,896]{1,0:T(8,128)(2,1)} %bitcast.99), channel_id=1, source_target_pairs={{0,4},{4,0},{8,12},{12,8},{16,20},{20,16},{24,28},{28,24},{1,5},{5... | collective-permute-start | bytes 11010056 | tf_op jit(solution)/shard_map/ppermute | solution.py:39
  273.6 111.4 %collective-permute-start.2 = (bf16[4,896,512]{1,2,0:T(8,128)(2,1)}, bf16[4,896,512]{1,2,0:T(8,128)(2,1)}, u32[]{:S(2)}, u32[]{:S(2)}) collective-permute-start(bf16[4,896,512]{1,2,0:T(8,128)(2,1)} %all-to-all-done.2), channel_id=1, source_target_pairs={{0,4},{4,0},{8,12},{12,8},{16,20},{20,16},{24,28},{28,24},{1,5},{5... | collective-permute-start | bytes 11010056 | tf_op jit(solution)/shard_map/ppermute | solution.py:39
  355.1 34.3 %collective-permute-start.1 = (bf16[2048,896]{1,0:T(8,128)(2,1)}, bf16[2048,896]{1,0:T(8,128)(2,1)}, u32[]{:S(2)}, u32[]{:S(2)}) collective-permute-start(bf16[2048,896]{1,0:T(8,128)(2,1)} %bitcast.102), channel_id=1, source_target_pairs={{0,4},{4,0},{8,12},{12,8},{16,20},{20,16},{24,28},{28,24},{1,5},{5... | collective-permute-start | bytes 11010056 | tf_op jit(solution)/shard_map/ppermute | solution.py:39
  368.1 3.3 copy-start.2
  371.4 2.3 copy-start.3
  373.7 2.4 copy-start.1
  406.6 53.2 %all-to-all-start.3 = ((bf16[4,512,1024]{1,2,0:T(8,128)(2,1)}), bf16[4,512,1024]{1,2,0:T(8,128)(2,1)}, u32[]{:S(2)}, u32[]{:S(2)}) async-start(bf16[4,512,1024]{1,2,0:T(8,128)(2,1)} %bitcast.86), calls=%async_computation.3 | async-start | bytes 8388608 | tf_op jit(solution)/shard_map/all_to_all | solution.py:108
  415.9 4.6 copy-start.4
  459.9 52.4 %all-to-all-start.5 = ((bf16[4,512,1024]{1,2,0:T(8,128)(2,1)}), bf16[4,512,1024]{1,2,0:T(8,128)(2,1)}, u32[]{:S(2)}, u32[]{:S(2)}) async-start(bf16[4,512,1024]{1,2,0:T(8,128)(2,1)} %bitcast.87), calls=%async_computation.5 | async-start | bytes 8388608 | tf_op jit(solution)/shard_map/all_to_all | solution.py:108
  512.2 28.7 %all-to-all-start.4 = ((bf16[4,128,1024]{2,1,0:T(8,128)(2,1)}), bf16[4,128,1024]{2,1,0:T(8,128)(2,1)S(1)}, u32[]{:S(2)}, u32[]{:S(2)}) async-start(bf16[4,128,1024]{2,1,0:T(8,128)(2,1)} %bitcast.22), calls=%async_computation.4 | async-start | bytes 2097152 | tf_op jit(solution)/shard_map/all_to_all | solution.py:36
  541.0 28.8 %all-to-all-start.6 = ((bf16[4,128,1024]{2,1,0:T(8,128)(2,1)}), bf16[4,128,1024]{2,1,0:T(8,128)(2,1)S(1)}, u32[]{:S(2)}, u32[]{:S(2)}) async-start(bf16[4,128,1024]{2,1,0:T(8,128)(2,1)} %bitcast.34), calls=%async_computation.6 | async-start | bytes 2097152 | tf_op jit(solution)/shard_map/all_to_all | solution.py:36
  570.0 23.1 %collective-permute-start.3 = (bf16[128,2048]{1,0:T(8,128)(2,1)S(1)}, bf16[128,2048]{1,0:T(8,128)(2,1)S(1)}, u32[]{:S(2)}, u32[]{:S(2)}) collective-permute-start(bf16[128,2048]{1,0:T(8,128)(2,1)S(1)} %pad_maximum_fusion.3), channel_id=1, source_target_pairs={{0,16},{4,20},{8,24},{12,28},{16,0},{20,4},{24,8},{28,12},{1,17},{... | collective-permute-start | bytes 1572872 | tf_op jit(solution)/shard_map/ppermute | solution.py:122
Sparse Core Ops, SparseCore 0:
  9.7 155.9 all-gather.3
  170.6 50.7 all-gather.7
  223.3 52.5 all-gather.5
